TPU v7x, 512 devices: a whole 4x4x16 slice. The times are simulated.
512 devices in a mesh: dp: 8 (over z_hi, y), expert: 64 (over z_lo, x, core).
Axes of the slice: x: 4, y: 4, z: 16 (z_hi: 2, z_lo: 8; z = z_hi * 8 + z_lo), core: 2. Of those that a mesh axis runs over, the one named last changes fastest.
Arguments:
- hidden_rows: bfloat16 [768, 65536], P(None, ('dp', 'expert')), may hold values from -6 to 6
- grad_rows: bfloat16 [65536, 2560], P(('dp', 'expert')), may hold values from -0.1796875 to 0.1796875
- block_slot: int32 [512, 1], P(('dp', 'expert')), may hold values from 0 to 1
- live_rows: int32 [512], P(('dp', 'expert')), may hold values from 16 to 128
- replica_plan: int32 [64], replicated, may hold values from 0 to 15
- master: float32 [64, 768, 640], P('expert', 'dp'), may hold values from -0.21875 to 0.21875
- moment_one: float32 [64, 768, 640], P('expert', 'dp'), may hold values from -1.8 to 1.8
- moment_two: float32 [64, 768, 640], P('expert', 'dp'), may hold values from 0.01 to 1
Outputs:
- master_new: float32 [64, 768, 640], P('expert', 'dp')
- first_new: float32 [64, 768, 640], P('expert', 'dp')
- second_new: float32 [64, 768, 640], P('expert', 'dp')
- replica_weight: bfloat16 [64, 768, 2560], P('expert', 'dp')
Inputs may be any that keep to these rules, and one draw needn't show every extreme that they name: replica_plan[j] is the expert of which the devices at index j along the expert axis host a replica; it may equal j mod 16. `block_slot`: 0 marks a block of the primary expert, 1 a block of the replica.
All inputs are finite; a program needn't handle non-finite values.
Results may differ from a plain program's by a relative error of at most 0.001.
Values may be sent and summed in bfloat16 or wider, within the bound.
A program may use at most 64 MiB of HBM per device.

v0:
```python
import jax
import jax.numpy as jnp
from jax import lax
from jax.sharding import PartitionSpec as P

QUART = 4
beta_one = 0.9
beta_two = 0.95
learn_rate = 0.01
decay_rate = 0.1
epsilon = 1e-08
step_count = 10.0


def from_behind(block, axis, distance):
    devices = range(lax.axis_size(axis))
    route = [((i - distance) % len(devices), i) for i in devices]
    return lax.ppermute(block, axis, route)


def adam_update(weights, first, second, gradient):
    first_next = beta_one * first + (1.0 - beta_one) * gradient
    second_next = beta_two * second + (1.0 - beta_two) * gradient * gradient
    scaled_first = first_next / (1.0 - beta_one**step_count)
    scaled_second = second_next / (1.0 - beta_two**step_count)
    direction = scaled_first / (jnp.sqrt(scaled_second) + epsilon)
    weights_next = weights - learn_rate * (direction + decay_rate * weights)
    return (weights_next, first_next, second_next)


def per_device(
    hidden_rows, grad_rows, block_slot, live_rows, replica_plan, master, moment_one, moment_two
):
    expert_count = lax.axis_size("expert")
    group_count = lax.axis_size("dp")
    own_index = lax.axis_index("expert")
    group_index = lax.axis_index("dp")
    hidden_units, tok_rows = hidden_rows.shape
    model_width = grad_rows.shape[1]
    block_count = block_slot.shape[1]
    block_span = tok_rows // block_count
    owner_count = expert_count // QUART
    block_width = model_width // QUART
    share_rows = hidden_units // group_count
    own_block = own_index // owner_count
    kept_rows = lax.iota(jnp.int32, tok_rows) < live_rows[0]
    row_slot = jnp.repeat(block_slot[0], block_span)
    zero_rows = jnp.zeros_like(grad_rows)
    grad_primary = jnp.where((kept_rows & (row_slot == 0))[:, None], grad_rows, zero_rows)
    grad_replica = jnp.where((kept_rows & (row_slot == 1))[:, None], grad_rows, zero_rows)
    replica_terms = jnp.dot(hidden_rows, grad_replica, preferred_element_type=jnp.float32).astype(
        jnp.bfloat16
    )
    primary_part = jnp.dot(hidden_rows, grad_primary, preferred_element_type=jnp.float32).reshape(
        hidden_units, QUART, block_width
    )
    primary_owned = lax.dynamic_index_in_dim(primary_part, own_block, 1, False)
    for step in range(1, QUART):
        target = (own_block + step) % QUART
        piece = lax.dynamic_index_in_dim(primary_part, target, 1, False)
        primary_owned = primary_owned + from_behind(piece, "expert", step * owner_count)
    expert_ids = lax.iota(jnp.int32, owner_count)
    holders = (replica_plan[None, :] == expert_ids[:, None]).astype(jnp.bfloat16)
    sectioned = replica_terms.reshape(
        expert_count, hidden_units // expert_count, QUART, block_width
    )
    pieces = lax.all_to_all(sectioned, "expert", split_axis=0, concat_axis=0, tiled=True)
    summed = jnp.einsum("es,skqd->qekd", holders, pieces, preferred_element_type=jnp.float32)
    summed = summed.reshape(expert_count, pieces.shape[1], pieces.shape[3])
    owned = lax.all_to_all(summed, "expert", split_axis=0, concat_axis=0, tiled=True).reshape(
        hidden_units, block_width
    )
    group_part = primary_owned + owned
    group_total = lax.psum(group_part, "dp")
    gradient = lax.dynamic_slice_in_dim(group_total, group_index * share_rows, share_rows, 0)
    weights_next, first_next, second_next = adam_update(
        master[0], moment_one[0], moment_two[0], gradient
    )
    fresh = weights_next.astype(jnp.bfloat16)
    chooser = (replica_plan[:, None] == expert_ids[None, :]).astype(jnp.bfloat16)
    sectioned_fresh = fresh.reshape(expert_count, 1, share_rows * block_width // expert_count)
    pieces = lax.all_to_all(sectioned_fresh, "expert", split_axis=0, concat_axis=0, tiled=True)
    grouped = pieces.reshape(QUART, owner_count, pieces.shape[1], pieces.shape[2])
    chosen = jnp.einsum(
        "je,qekc->jkqc", chooser, grouped, preferred_element_type=jnp.float32
    ).astype(jnp.bfloat16)
    received = lax.all_to_all(chosen, "expert", split_axis=0, concat_axis=0, tiled=True)
    blocks = jnp.transpose(received[:, 0], (1, 0, 2)).reshape(QUART, share_rows, block_width)
    replica_weight = jnp.transpose(blocks, (1, 0, 2)).reshape(share_rows, model_width)
    return (weights_next[None], first_next[None], second_next[None], replica_weight[None])


def solution(mesh):
    return jax.shard_map(
        per_device,
        mesh=mesh,
        in_specs=(
            P(None, ("dp", "expert")),
            P(("dp", "expert"), None),
            P(("dp", "expert"), None),
            P(("dp", "expert")),
            P(),
            P("expert", "dp", None),
            P("expert", "dp", None),
            P("expert", "dp", None),
        ),
        out_specs=(
            P("expert", "dp", None),
            P("expert", "dp", None),
            P("expert", "dp", None),
            P("expert", "dp", None),
        ),
        check_vma=False,
    )
```

profile of v0, /device:TPU:25, one launch (start us, length us, event | category | flops | bytes accessed | tf_op | source)
XLA Modules:
  0.0 986.9 jit_solution(8224352198364253314)
XLA Ops:
  7.2 0.0 copy-start
  8.5 0.0 copy-done
  8.5 4.3 fusion
  12.8 6.4 copy.50
  19.2 7.6 reshape.58
  26.8 0.0 copy-start.5
  26.8 190.7 %all_to_all.20 = bf16[64,12,4,640]{3,2,1,0:T(4,128)(2,1)S(1)} all-to-all(bf16[64,12,4,640]{3,2,1,0:T(4,128)(2,1)} %reshape.58), channel_id=1, replica_groups=mesh['dp'=8,'expert'=64] {'expert'}, dimensions={0} | all-to-all | bytes 7864320 | tf_op jit(solution)/shard_map/all_to_all | solution.py:67
  217.5 0.0 copy-done.5
  217.5 0.7 fusion.1
  218.1 2.7 copy.52
  220.8 0.0 copy-start.1
  220.8 8.7 all-to-all-start.1
  229.5 0.0 all-reduce.2.cloned.1.call-start
  229.6 0.0 copy-done.1
  229.6 1.3 fusion.8
  230.9 3.2 constant_dynamic-slice_fusion.3
  234.2 2.9 copy.47
  237.1 4.2 collective-permute-start
  241.2 2.9 copy.48
  244.1 7.2 collective-permute-start.1
  251.3 2.9 copy.49
  254.2 5.1 collective-permute-start.2
  259.2 2.9 copy.46
  262.1 276.0 %all-to-all-done.1 = f32[64,12,640]{2,1,0:T(8,128)S(1)} async-done(((f32[64,12,640]{2,1,0:T(8,128)}), f32[64,12,640]{2,1,0:T(8,128)S(1)}, u32[]{:S(2)}, u32[]{:S(2)}) %all-to-all-start.1) | async-done | bytes 1966112 | tf_op jit(solution)/shard_map/all_to_all | solution.py:70
  538.1 1.4 reshape.60
  539.5 0.0 collective-permute-done
  539.5 103.2 %collective-permute-done.1 = f32[768,640]{1,0:T(8,128)} collective-permute-done((f32[768,640]{1,0:T(8,128)}, f32[768,640]{1,0:T(8,128)}, u32[]{:S(2)}, u32[]{:S(2)}) %collective-permute-start.1) | collective-permute-done | bytes 1966112 | tf_op jit(solution)/shard_map/ppermute | solution.py:18
  642.8 0.0 collective-permute-done.2
  642.8 5.6 fusion.5
  648.4 0.0 copy-start.2
  648.4 0.0 copy-start.3
  648.4 0.0 copy-start.4
  648.4 0.0 all-reduce.2.cloned.1.call-update
  648.4 264.2 %all-reduce.2.cloned.1.call-done = f32[768,640]{1,0:T(8,128)} async-done(((f32[768,640]{1,0:T(8,128)}), f32[768,640]{1,0:T(8,128)}) %all-reduce.2.cloned.1.call-update) | async-done | bytes 1966096 | tf_op jit(solution)/shard_map/psum | solution.py:74
  912.6 0.0 copy-done.2
  912.6 0.0 copy-done.3
  912.6 0.0 copy-done.4
  912.6 1.9 fusion.27
  914.5 0.2 reshape.66
  914.7 0.5 broadcast.46
  915.2 1.4 reduce
  916.7 0.2 reshape.68
  916.8 24.4 %all_to_all.21 = bf16[64,2,480]{2,1,0:T(2,128)(2,1)S(1)} all-to-all(bf16[64,2,480]{2,1,0:T(2,128)(2,1)S(1)} %reshape.68), channel_id=1, replica_groups=mesh['dp'=8,'expert'=64] {'expert'}, dimensions={0} | all-to-all | bytes 245760 | tf_op jit(solution)/shard_map/all_to_all | solution.py:82
  941.2 0.2 reshape.69
  941.5 0.3 fusion.6
  941.8 0.4 copy.54
  942.2 35.7 %all_to_all.22 = bf16[64,1,4,960]{3,2,1,0:T(4,128)(2,1)S(1)} all-to-all(bf16[64,1,4,960]{3,2,1,0:T(4,128)(2,1)S(1)} %copy.54), channel_id=1, replica_groups=mesh['dp'=8,'expert'=64] {'expert'}, dimensions={0} | all-to-all | bytes 983040 | tf_op jit(solution)/shard_map/all_to_all | solution.py:87
  977.9 0.2 copy.55
  978.1 0.8 reshape.63
  978.9 0.3 copy.56
  979.1 1.0 broadcast_in_dim_reshape.3
  (2 shorter events, 0.1 us)
Async XLA Ops:
  7.2 1.4 copy-start
  26.8 190.7 %copy-start.5 = (s32[64]{0:T(128)S(1)}, s32[64]{0:T(128)}, u32[]{:S(2)}) copy-start(s32[64]{0:T(128)} %param.12) | copy-start | bytes 772
  220.8 8.8 copy-start.1
  220.8 317.3 %all-to-all-start.1 = ((f32[64,12,640]{2,1,0:T(8,128)}), f32[64,12,640]{2,1,0:T(8,128)S(1)}, u32[]{:S(2)}, u32[]{:S(2)}) async-start(f32[64,12,640]{2,1,0:T(8,128)} %copy.52), calls=%async_computation.1 | async-start | bytes 5242880 | tf_op jit(solution)/shard_map/all_to_all | solution.py:70
  229.5 683.1 %all-reduce.2.cloned.1.call-start = ((), (), s32[]{:S(2)}) async-start(), calls=%async_computation.4 | async-start | bytes 3932160 | tf_op jit(solution)/shard_map/psum | solution.py:74
  237.1 302.5 %collective-permute-start = (f32[768,640]{1,0:T(8,128)}, f32[768,640]{1,0:T(8,128)}, u32[]{:S(2)}, u32[]{:S(2)}) collective-permute-start(f32[768,640]{1,0:T(8,128)} %bitcast.75), channel_id=1, source_target_pairs={{48,0},{49,1},{50,2},{51,3},{52,4},{53,5},{54,6},{55,7},{56,8},{57... | collective-permute-start | bytes 5898248 | tf_op jit(solution)/shard_map/ppermute | solution.py:18
  244.1 398.7 %collective-permute-start.1 = (f32[768,640]{1,0:T(8,128)}, f32[768,640]{1,0:T(8,128)}, u32[]{:S(2)}, u32[]{:S(2)}) collective-permute-start(f32[768,640]{1,0:T(8,128)} %bitcast.76), channel_id=1, source_target_pairs={{32,0},{33,1},{34,2},{35,3},{36,4},{37,5},{38,6},{39,7},{40,8},{41... | collective-permute-start | bytes 5898248 | tf_op jit(solution)/shard_map/ppermute | solution.py:18
  254.2 388.6 %collective-permute-start.2 = (f32[768,640]{1,0:T(8,128)}, f32[768,640]{1,0:T(8,128)}, u32[]{:S(2)}, u32[]{:S(2)}) collective-permute-start(f32[768,640]{1,0:T(8,128)} %bitcast.77), channel_id=1, source_target_pairs={{16,0},{17,1},{18,2},{19,3},{20,4},{21,5},{22,6},{23,7},{24,8},{25... | collective-permute-start | bytes 5898248 | tf_op jit(solution)/shard_map/ppermute | solution.py:18
  648.4 264.2 %copy-start.2 = (f32[1,96,640]{2,1,0:T(8,128)S(1)}, f32[1,96,640]{2,1,0:T(8,128)}, u32[]{:S(2)}) copy-start(f32[1,96,640]{2,1,0:T(8,128)} %param.15) | copy-start | bytes 737284
  648.4 264.2 %copy-start.3 = (f32[1,96,640]{2,1,0:T(8,128)S(1)}, f32[1,96,640]{2,1,0:T(8,128)}, u32[]{:S(2)}) copy-start(f32[1,96,640]{2,1,0:T(8,128)} %param.14) | copy-start | bytes 737284
  648.4 264.2 %copy-start.4 = (f32[1,96,640]{2,1,0:T(8,128)S(1)}, f32[1,96,640]{2,1,0:T(8,128)}, u32[]{:S(2)}) copy-start(f32[1,96,640]{2,1,0:T(8,128)} %param.13) | copy-start | bytes 737284
Sparse Core Ops, SparseCore 0:
  648.5 264.0 all-reduce.1
where the time goes:
time: 988 us; the launch traced here: 987 us
  waiting for transfers between devices  643 us (65%)
  blocking collectives  251 us (25%)
  local copies, waits for them, and re-layouts  36.5 us (4%)
  starting transfers between devices  25.1 us (3%)
  between operations  15.6 us (2%)
    all_to_all x1, waiting for transfers between devices, per_device(): lax.all_to_all(summed, 'expert', split_axis=0, concat_axis=0, tiled=True)  276 us
    psum x1, waiting for transfers between devices, per_device(): group_total = lax.psum(group_part, 'dp')  264 us
    all_to_all x1, blocking collectives, per_device(): lax.all_to_all(sectioned, 'expert', split_axis=0, concat_axis=0, tiled=True)  191 us
    ppermute x3, waiting for transfers between devices, from_behind(): return lax.ppermute(block, axis, route)  103 us
    all_to_all x1, blocking collectives, per_device(): lax.all_to_all(chosen, 'expert', split_axis=0, concat_axis=0, tiled=True)  35.7 us
    all_to_all x1, blocking collectives, per_device(): lax.all_to_all(sectioned_fresh, 'expert', split_axis=0, concat_axis=0, ti...  24.4 us
  transfers between devices with their start and end apart: 5, of which 3 were waited for; matrix products, arithmetic and copies ran while one was open for 2% of the time, Pallas kernels for 0%

commit v1 on v0

--- a/solution.py
+++ b/solution.py
@@ -71,7 +71,8 @@
         hidden_units, block_width
     )
     group_part = primary_owned + owned
-    group_total = lax.psum(group_part, "dp")
+    parts = lax.all_gather(group_part, "dp")
+    group_total = jnp.sum(parts, axis=0)
     gradient = lax.dynamic_slice_in_dim(group_total, group_index * share_rows, share_rows, 0)
     weights_next, first_next, second_next = adam_update(
         master[0], moment_one[0], moment_two[0], gradient

time: 988 us -> 1280 us (1.30)
  waiting for transfers between devices: 643 us -> 908 us
  blocking collectives: 251 us -> 272 us
    all_gather x0 -> x1, waiting for transfers between devices: none -> 529 us  [per_device(): parts = lax.all_gather(group_part, 'dp')]
    psum x1 -> x0, waiting for transfers between devices: 264 us -> none  [per_device(): group_total = lax.psum(group_part, 'dp')]
    all_to_all x1, blocking collectives: 24.4 us -> 45.4 us  [per_device(): lax.all_to_all(sectioned_fresh, 'expert', split_axis=0, concat_axis=0, ti...]
  transfers between devices with their start and end apart: 5 -> 5, of which waited for: 3 -> 3; matrix products, arithmetic and copies ran while one was open for 2% -> 1% of each run, Pallas kernels for 0% -> 0%
where the time goes in v1:
time: 1280 us
  waiting for transfers between devices  908 us (71%)
  blocking collectives  272 us (21%)
  local copies, waits for them, and re-layouts  36.4 us (3%)
  starting transfers between devices  25.3 us (2%)
  between operations  15.6 us (1%)
  other arithmetic  14.6 us (1%)
    all_gather x1, waiting for transfers between devices, per_device(): parts = lax.all_gather(group_part, 'dp')  529 us
    all_to_all x1, waiting for transfers between devices, per_device(): lax.all_to_all(summed, 'expert', split_axis=0, concat_axis=0, tiled=True)  276 us
    all_to_all x1, blocking collectives, per_device(): lax.all_to_all(sectioned, 'expert', split_axis=0, concat_axis=0, tiled=True)  191 us
    ppermute x3, waiting for transfers between devices, from_behind(): return lax.ppermute(block, axis, route)  103 us
    all_to_all x1, blocking collectives, per_device(): lax.all_to_all(sectioned_fresh, 'expert', split_axis=0, concat_axis=0, ti...  45.4 us
    all_to_all x1, blocking collectives, per_device(): lax.all_to_all(chosen, 'expert', split_axis=0, concat_axis=0, tiled=True)  35.7 us
  transfers between devices with their start and end apart: 5, of which 3 were waited for; matrix products, arithmetic and copies ran while one was open for 1% of the time, Pallas kernels for 0%

profile of v1, /device:TPU:25, one launch (start us, length us, event | category | flops | bytes accessed | tf_op | source)
XLA Modules:
  0.0 1278.4 jit_solution(2905322084862689778)
XLA Ops:
  7.2 0.0 copy-start
  8.5 0.0 copy-done
  8.5 4.3 fusion
  12.8 6.3 copy.44
  19.1 7.6 reshape.58
  26.7 0.0 copy-start.6
  26.7 190.7 %all_to_all.20 = bf16[64,12,4,640]{3,2,1,0:T(4,128)(2,1)S(1)} all-to-all(bf16[64,12,4,640]{3,2,1,0:T(4,128)(2,1)} %reshape.58), channel_id=1, replica_groups=mesh['dp'=8,'expert'=64] {'expert'}, dimensions={0} | all-to-all | bytes 7864320 | tf_op jit(solution)/shard_map/all_to_all | solution.py:67
  217.4 0.0 copy-done.6
  217.4 0.7 fusion.1
  218.1 2.7 copy.46
  220.8 0.0 copy-start.2
  220.8 8.7 all-to-all-start.1
  229.5 0.0 all-gather.3.cloned.1.call-start
  229.6 0.0 copy-done.2
  229.6 1.3 fusion.8
  230.9 3.2 constant_dynamic-slice_fusion.3
  234.1 2.9 copy.41
  237.0 4.2 collective-permute-start
  241.2 2.9 copy.42
  244.1 7.2 collective-permute-start.1
  251.3 2.9 copy.43
  254.1 5.3 collective-permute-start.2
  259.4 2.8 copy.40
  262.2 275.9 %all-to-all-done.1 = f32[64,12,640]{2,1,0:T(8,128)S(1)} async-done(((f32[64,12,640]{2,1,0:T(8,128)}), f32[64,12,640]{2,1,0:T(8,128)S(1)}, u32[]{:S(2)}, u32[]{:S(2)}) %all-to-all-start.1) | async-done | bytes 1966112 | tf_op jit(solution)/shard_map/all_to_all | solution.py:70
  538.1 1.4 reshape.60
  539.5 0.0 collective-permute-done
  539.5 103.2 %collective-permute-done.1 = f32[768,640]{1,0:T(8,128)} collective-permute-done((f32[768,640]{1,0:T(8,128)}, f32[768,640]{1,0:T(8,128)}, u32[]{:S(2)}, u32[]{:S(2)}) %collective-permute-start.1) | collective-permute-done | bytes 1966112 | tf_op jit(solution)/shard_map/ppermute | solution.py:18
  642.7 0.0 collective-permute-done.2
  642.7 5.6 fusion.5
  648.3 0.0 all-gather.3.cloned.1.call-update
  648.3 529.0 %all-gather.3.cloned.1.call-done = f32[6144,640]{1,0:T(8,128)} async-done(((f32[768,640]{1,0:T(8,128)}), f32[6144,640]{1,0:T(8,128)}) %all-gather.3.cloned.1.call-update) | async-done | bytes 15728656 | tf_op jit(solution)/shard_map/all_gather | solution.py:74
  1177.3 0.0 copy-start.3
  1177.3 0.0 copy-start.4
  1177.3 0.0 copy-start.5
  1177.3 6.6 reduce_sum.9
  1184.0 0.0 copy-done.3
  1184.0 0.0 copy-done.4
  1184.0 0.0 copy-done.5
  1184.0 1.0 fusion.27
  1185.0 0.2 reshape.67
  1185.2 0.5 broadcast.46
  1185.7 1.4 reduce
  1187.1 0.2 reshape.69
  1187.3 45.4 %all_to_all.21 = bf16[64,2,480]{2,1,0:T(2,128)(2,1)S(1)} all-to-all(bf16[64,2,480]{2,1,0:T(2,128)(2,1)S(1)} %reshape.69), channel_id=1, replica_groups=mesh['dp'=8,'expert'=64] {'expert'}, dimensions={0} | all-to-all | bytes 245760 | tf_op jit(solution)/shard_map/all_to_all | solution.py:83
  1232.7 0.2 reshape.70
  1232.9 0.3 fusion.6
  1233.3 0.4 copy.48
  1233.7 35.7 %all_to_all.22 = bf16[64,1,4,960]{3,2,1,0:T(4,128)(2,1)S(1)} all-to-all(bf16[64,1,4,960]{3,2,1,0:T(4,128)(2,1)S(1)} %copy.48), channel_id=1, replica_groups=mesh['dp'=8,'expert'=64] {'expert'}, dimensions={0} | all-to-all | bytes 983040 | tf_op jit(solution)/shard_map/all_to_all | solution.py:88
  1269.4 0.0 copy-start.1
  1269.4 0.2 copy.49
  1269.5 0.8 reshape.63
  1270.3 0.3 copy.50
  1270.6 1.0 broadcast_in_dim_reshape.3
  1271.5 0.0 copy-done.1
  (2 shorter events, 0.1 us)
Async XLA Ops:
  7.2 1.4 copy-start
  26.7 190.7 %copy-start.6 = (s32[64]{0:T(128)S(1)}, s32[64]{0:T(128)}, u32[]{:S(2)}) copy-start(s32[64]{0:T(128)} %param.12) | copy-start | bytes 772
  220.8 8.8 copy-start.2
  220.8 317.3 %all-to-all-start.1 = ((f32[64,12,640]{2,1,0:T(8,128)}), f32[64,12,640]{2,1,0:T(8,128)S(1)}, u32[]{:S(2)}, u32[]{:S(2)}) async-start(f32[64,12,640]{2,1,0:T(8,128)} %copy.46), calls=%async_computation.1 | async-start | bytes 5242880 | tf_op jit(solution)/shard_map/all_to_all | solution.py:70
  229.5 947.9 %all-gather.3.cloned.1.call-start = ((), (), s32[]{:S(2)}) async-start(), calls=%async_computation.4 | async-start | bytes 17694720 | tf_op jit(solution)/shard_map/all_gather | solution.py:74
  237.0 302.5 %collective-permute-start = (f32[768,640]{1,0:T(8,128)}, f32[768,640]{1,0:T(8,128)}, u32[]{:S(2)}, u32[]{:S(2)}) collective-permute-start(f32[768,640]{1,0:T(8,128)} %bitcast.77), channel_id=1, source_target_pairs={{48,0},{49,1},{50,2},{51,3},{52,4},{53,5},{54,6},{55,7},{56,8},{57... | collective-permute-start | bytes 5898248 | tf_op jit(solution)/shard_map/ppermute | solution.py:18
  244.1 398.7 %collective-permute-start.1 = (f32[768,640]{1,0:T(8,128)}, f32[768,640]{1,0:T(8,128)}, u32[]{:S(2)}, u32[]{:S(2)}) collective-permute-start(f32[768,640]{1,0:T(8,128)} %bitcast.78), channel_id=1, source_target_pairs={{32,0},{33,1},{34,2},{35,3},{36,4},{37,5},{38,6},{39,7},{40,8},{41... | collective-permute-start | bytes 5898248 | tf_op jit(solution)/shard_map/ppermute | solution.py:18
  254.1 388.6 %collective-permute-start.2 = (f32[768,640]{1,0:T(8,128)}, f32[768,640]{1,0:T(8,128)}, u32[]{:S(2)}, u32[]{:S(2)}) collective-permute-start(f32[768,640]{1,0:T(8,128)} %bitcast.79), channel_id=1, source_target_pairs={{16,0},{17,1},{18,2},{19,3},{20,4},{21,5},{22,6},{23,7},{24,8},{25... | collective-permute-start | bytes 5898248 | tf_op jit(solution)/shard_map/ppermute | solution.py:18
  1177.3 6.6 copy-start.3
  1177.3 6.6 copy-start.4
  1177.3 6.7 copy-start.5
  1269.4 2.2 copy-start.1
Sparse Core Ops, SparseCore 0:
  648.5 528.8 all-gather.2
